TPU v7x, 32 devices: a whole 2x2x4 slice. The times are simulated.
32 devices in a mesh: band: 4 (over x, core), lev: 8 (over z, y).
Axes of the slice: x: 2, y: 2, z: 4, core: 2. Of those that a mesh axis runs over, the one named last changes fastest.
Arguments:
- grid_in: bfloat16 [3, 32, 16, 2688], P(None, 'lev', 'band'), may hold values from -6 to 6
- row_shift: int32 [16], P('band'), may hold values from -3 to 0
- block_shift: int32 [16], P('band'), may hold values from 0 to 20
- interp_weights: bfloat16 [16, 4, 3, 128, 128], P('band'), may hold values from -0.15625 to 0.15625
- wave_order: int32 [128], replicated, may hold values from 0 to 127, as said below
- legendre: bfloat16 [128, 16, 1280], P('band'), may hold values from -1.5 to 1.5
Outputs:
- spectral: bfloat16 [3, 32, 128, 2, 1280], P(None, 'lev', 'band')
Inputs may be any that keep to these rules, and one draw needn't show every extreme that they name: `row_shift`: each latitude's stencil rows lie within 3 rows of it on both sides. `wave_order`: a permutation of the 128 wavenumbers; slots d * 32 to (d + 1) * 32 - 1 hold exactly one wavenumber of each aligned run of 4 consecutive wavenumbers.
All inputs are finite; a program needn't handle non-finite values.
Results may differ from a plain program's by a relative error of at most 0.0065.
Values may be sent and summed in bfloat16 or wider, within the bound.
A program may use at most 128 MiB of HBM per device.

v0:
```python
import math
import jax
import jax.numpy as jnp
from jax import lax
from jax.sharding import PartitionSpec as P

BLK = 128
HALO = 3
STENCIL = 4


def with_halo(block, sides, width):
    for axis, dim in sides:
        count = lax.axis_size(axis)
        forward = [(i, i + 1) for i in range(count - 1)]
        backward = [(target, source) for source, target in forward]
        low = lax.ppermute(
            lax.slice_in_dim(block, block.shape[dim] - width, None, axis=dim), axis, forward
        )
        high = lax.ppermute(lax.slice_in_dim(block, 0, width, axis=dim), axis, backward)
        block = jnp.concatenate([low, block, high], axis=dim)
    return block


def make_table(waves, longitudes):
    column = jnp.arange(longitudes, dtype=jnp.int32)[:, None]
    phase = column * waves[None, :] % longitudes
    angle = phase.astype(jnp.float32) * (2.0 * math.pi / longitudes)
    paired = jnp.stack([jnp.cos(angle), -jnp.sin(angle)], axis=2)
    return (paired.reshape(longitudes, 2 * waves.shape[0]) / math.sqrt(longitudes)).astype(
        jnp.bfloat16
    )


def stencil_rows(source, row_index, row_shift, block_shift):
    start = row_index + HALO + row_shift[row_index]
    rows = lax.dynamic_slice_in_dim(source, start, STENCIL, 2)
    rows = jnp.roll(rows, -block_shift[row_index] * BLK, axis=3)
    return rows.reshape(rows.shape[0], rows.shape[1], STENCIL, rows.shape[3] // BLK, BLK)


def vertical_terms(rows, weights, depth):
    total = None
    for level_step in range(3):
        term = jnp.einsum(
            "flsbj,sji->flbi",
            rows[:, level_step : level_step + depth],
            weights[:, level_step],
            preferred_element_type=jnp.float32,
        )
        total = term if total is None else total + term
    return total.reshape(total.shape[0], total.shape[1], total.shape[2] * total.shape[3])


def per_device(grid_in, row_shift, block_shift, interp_weights, wave_order, legendre):
    fields, depth, lat_rows, longitudes = grid_in.shape
    owned, latitudes, degrees = legendre.shape
    widened = with_halo(grid_in, (("band", 2),), HALO)
    extended = with_halo(widened, (("lev", 1),), 1)
    pieces = []
    for row_index in range(lat_rows):
        rows = stencil_rows(extended, row_index, row_shift, block_shift)
        pieces.append(vertical_terms(rows, interp_weights[row_index], depth))
    combined = jnp.stack(pieces, axis=2)
    interp = combined.astype(jnp.bfloat16)
    items = fields * depth
    own_waves = lax.dynamic_slice_in_dim(wave_order, lax.axis_index("band") * owned, owned)
    degree = jnp.arange(degrees, dtype=jnp.int32)[None, :]
    keep = degree >= own_waves[:, None]
    table = make_table(wave_order, longitudes)
    fourier = jnp.dot(
        interp.reshape(items * lat_rows, longitudes), table, preferred_element_type=jnp.float32
    )
    fourier = fourier.astype(jnp.bfloat16).reshape(items, lat_rows, table.shape[1])
    coeffs = lax.all_to_all(fourier, "band", split_axis=2, concat_axis=1, tiled=True)
    shaped = coeffs.reshape(coeffs.shape[0], latitudes, owned, 2)
    result = jnp.einsum("arqc,qrn->aqcn", shaped, legendre, preferred_element_type=jnp.float32)
    result = jnp.where(keep[None, :, None, :], result, jnp.zeros((), jnp.float32))
    spectral = result.astype(jnp.bfloat16)
    return spectral.reshape(fields, depth, owned, 2, degrees)


def solution(mesh):
    return jax.shard_map(
        per_device,
        mesh=mesh,
        in_specs=(
            P(None, "lev", "band", None),
            P("band"),
            P("band"),
            P("band", None, None, None, None),
            P(),
            P("band", None, None),
        ),
        out_specs=P(None, "lev", "band", None, None),
        check_vma=False,
    )
```

profile of v0, /device:TPU:8, one launch (start us, length us, event | category | flops | bytes accessed | tf_op | source)
XLA Modules:
  0.0 109.0 jit_solution(10730107957513051599)
XLA Ops:
  0.0 0.0 copy-start
  0.0 2.2 %fusion.27 = (bf16[3,4,3,2688]{3,2,1,0:T(4,128)(2,1)}, bf16[3,4,3,2688]{3,2,1,0:T(4,128)(2,1)}) fusion(bf16[3,4,4,2688]{3,2,1,0:T(4,128)(2,1)} %param.8), kind=kLoop, calls=%fused_computation.79 | loop fusion | bytes 774144 | tf_op jit(solution)/shard_map/slice | solution.py:18
  2.2 2.6 %collective-permute-start = (bf16[3,4,3,2688]{3,2,1,0:T(4,128)(2,1)}, bf16[3,4,3,2688]{3,2,1,0:T(4,128)(2,1)}, u32[]{:S(2)}, u32[]{:S(2)}) collective-permute-start(bf16[3,4,3,2688]{3,2,1,0:T(4,128)(2,1)} %get-tuple-element.16), channel_id=1, source_target_pairs={{0,8},{8,16},{16,24},{1,9},{9,17},{17,25},{2,10},{10,18},{18,26},{... | collective-permute-start | bytes 580616 | tf_op jit(solution)/shard_map/ppermute | solution.py:17
  4.8 1.3 %collective-permute-start.1 = (bf16[3,4,3,2688]{3,2,1,0:T(4,128)(2,1)}, bf16[3,4,3,2688]{3,2,1,0:T(4,128)(2,1)}, u32[]{:S(2)}, u32[]{:S(2)}) collective-permute-start(bf16[3,4,3,2688]{3,2,1,0:T(4,128)(2,1)} %get-tuple-element.17), channel_id=1, source_target_pairs={{8,0},{16,8},{24,16},{9,1},{17,9},{25,17},{10,2},{18,10},{26,18},{... | collective-permute-start | bytes 580616 | tf_op jit(solution)/shard_map/ppermute | solution.py:20
  6.1 1.5 %fusion.29 = (s32[1]{0:T(128)}, s32[1]{0:T(128)}, s32[1]{0:T(128)}, s32[1]{0:T(128)}) fusion(s32[4]{0:T(128)} %param.10), kind=kLoop, calls=%fused_computation.81 | loop fusion | bytes 32 | tf_op jit(solution)/shard_map/slice | solution.py:38
  10.2 7.3 %fusion.6 = (f32[2688,128,1]{1,0,2:T(8,128)S(1)}, f32[2688,128,1]{1,0,2:T(8,128)}) fusion(s32[128]{0:T(128)} %param.12), kind=kLoop, calls=%fused_computation.12 | loop fusion | flops 3440640 | bytes 2753024 | tf_op jit(solution)/shard_map/cos | solution.py:29
  17.5 0.0 copy-done.11
  17.5 0.1 dynamic_slice.18
  17.6 0.7 fusion.28
  23.5 0.0 copy-start.1
  23.5 2.5 %fusion.26 = (bf16[1,4,3,128,128]{4,3,2,1,0:T(8,128)(2,1)}, bf16[1,4,3,128,128]{4,3,2,1,0:T(8,128)(2,1)S(1)}, bf16[1,4,3,128,128]{4,3,2,1,0:T(8,128)(2,1)}, bf16[1,4,3,128,128]{4,3,2,1,0:T(8,128)(2,1)}) fusion(bf16[4,4,3,128,128]{4,3,2,1,0:T(8,128)(2,1)} %param.11), kind=kLoop, calls=%fused_computation.78 | loop fusion | bytes 3145728 | tf_op jit(solution)/shard_map/slice | solution.py:63
  26.1 1.4 %fusion.1 = bf16[2688,128,2]{1,0,2:T(8,128)(2,1)} fusion(f32[2688,128,1]{1,0,2:T(8,128)S(1)} %copy-done.1, f32[2688,128,1]{1,0,2:T(8,128)S(1)} %get-tuple-element.18), kind=kLoop, calls=%fused_computation.3 | loop fusion | flops 2064384 | bytes 4128768 | tf_op jit(solution)/shard_map/convert_element_type | solution.py:30
  27.4 4.8 %copy.57 = bf16[2688,128,2]{0,2,1:T(2,128)(2,1)} copy(bf16[2688,128,2]{1,0,2:T(8,128)(2,1)} %fusion.1) | data formatting | bytes 2752512 | tf_op jit(solution)/shard_map/convert_element_type | solution.py:30
  32.2 3.3 %convert_element_type.49 = bf16[2688,256]{0,1:T(8,128)(2,1)S(1)} reshape(bf16[2688,128,2]{0,2,1:T(2,128)(2,1)} %copy.57) | data formatting | bytes 2752512 | tf_op jit(solution)/shard_map/convert_element_type | solution.py:30
  35.6 2.1 %copy_bitcast_fusion.2 = (bf16[4,3,128,128]{3,2,0,1:T(8,128)(2,1)}, bf16[4,3,128,128]{3,2,0,1:T(8,128)(2,1)}) fusion(bf16[1,4,3,128,128]{4,3,2,1,0:T(8,128)(2,1)} %get-tuple-element.8, bf16[1,4,3,128,128]{4,3,2,1,0:T(8,128)(2,1)} %get-tuple-element.6), kind=kLoop, calls=%fused_computation.50 | loop fusion | bytes 1572864 | tf_op jit(solution)/shard_map/squeeze | solution.py:63
  37.7 0.0 collective-permute-done
  37.7 0.0 collective-permute-done.1
  37.7 0.0 copy-done.4
  37.7 1.2 %pad_maximum_fusion.3 = (bf16[3,1,10,2688]{3,2,1,0:T(8,128)(2,1)S(1)}, bf16[3,1,10,2688]{3,2,1,0:T(8,128)(2,1)S(1)}) fusion(bf16[3,4,3,2688]{3,2,1,0:T(4,128)(2,1)} %collective-permute-done.1, bf16[3,4,4,2688]{3,2,1,0:T(4,128)(2,1)S(1)} %copy-done.4, bf16[3,4,3,2688]{3,2,1,0:T(4,128)(2,1)} %collective-permute-done), kind=kLoop, calls=%fused_computation.59 | loop fusion | flops 967680 | bytes 967680 | tf_op jit(solution)/shard_map/slice | solution.py:18
  38.9 3.4 %collective-permute-start.2 = (bf16[3,1,10,2688]{3,2,1,0:T(8,128)(2,1)S(1)}, bf16[3,1,10,2688]{3,2,1,0:T(8,128)(2,1)S(1)}, u32[]{:S(2)}, u32[]{:S(2)}) collective-permute-start(bf16[3,1,10,2688]{3,2,1,0:T(8,128)(2,1)S(1)} %get-tuple-element.14), channel_id=1, source_target_pairs={{0,1},{1,2},{2,3},{3,4},{4,5},{5,6},{6,7},{8,9},{9,10},{10,11},{11... | collective-permute-start | bytes 483848 | tf_op jit(solution)/shard_map/ppermute | solution.py:17
  42.4 3.5 %collective-permute-start.3 = (bf16[3,1,10,2688]{3,2,1,0:T(8,128)(2,1)S(1)}, bf16[3,1,10,2688]{3,2,1,0:T(8,128)(2,1)S(1)}, u32[]{:S(2)}, u32[]{:S(2)}) collective-permute-start(bf16[3,1,10,2688]{3,2,1,0:T(8,128)(2,1)S(1)} %get-tuple-element.15), channel_id=1, source_target_pairs={{1,0},{2,1},{3,2},{4,3},{5,4},{6,5},{7,6},{9,8},{10,9},{11,10},{12... | collective-permute-start | bytes 483848 | tf_op jit(solution)/shard_map/ppermute | solution.py:20
  45.9 0.0 copy-done.5
  45.9 1.0 copy_bitcast_fusion
  46.9 6.8 %collective-permute-done.2 = bf16[3,1,10,2688]{3,2,1,0:T(8,128)(2,1)S(1)} collective-permute-done((bf16[3,1,10,2688]{3,2,1,0:T(8,128)(2,1)S(1)}, bf16[3,1,10,2688]{3,2,1,0:T(8,128)(2,1)S(1)}, u32[]{:S(2)}, u32[]{:S(2)}) %collective-permute-start.2) | collective-permute-done | bytes 161312 | tf_op jit(solution)/shard_map/ppermute | solution.py:17
  53.7 2.7 %collective-permute-done.3 = bf16[3,1,10,2688]{3,2,1,0:T(8,128)(2,1)S(1)} collective-permute-done((bf16[3,1,10,2688]{3,2,1,0:T(8,128)(2,1)S(1)}, bf16[3,1,10,2688]{3,2,1,0:T(8,128)(2,1)S(1)}, u32[]{:S(2)}, u32[]{:S(2)}) %collective-permute-start.3) | collective-permute-done | bytes 161312 | tf_op jit(solution)/shard_map/ppermute | solution.py:20
  56.3 1.7 %pad_maximum_fusion = bf16[3,6,10,2688]{3,2,1,0:T(8,128)(2,1)S(1)} fusion(bf16[3,1,10,2688]{3,2,1,0:T(8,128)(2,1)S(1)} %collective-permute-done.3, bf16[3,4,3,2688]{3,2,1,0:T(4,128)(2,1)} %collective-permute-done.1, bf16[3,4,4,2688]{3,2,1,0:T(4,128)(2,1)S(1)} %copy-done.4, bf16[3,4,3,2688]{3,2,1,0:T(4,128)(2,1)} %collective-permute-done, ...), kind=kLoop, calls=%fused_computation.5 | loop fusion | flops 4838400 | bytes 1935360 | tf_op jit(solution)/shard_map/concatenate | solution.py:21
  58.0 1.9 %constant_dynamic-slice_fusion.3 = (bf16[3,6,4,2688]{3,2,1,0:T(4,128)(2,1)S(1)}, bf16[3,6,4,2688]{3,2,1,0:T(4,128)(2,1)}, bf16[3,6,4,2688]{3,2,1,0:T(4,128)(2,1)}, bf16[3,6,4,2688]{3,2,1,0:T(4,128)(2,1)S(1)}) fusion(bf16[3,6,10,2688]{3,2,1,0:T(8,128)(2,1)S(1)} %pad_maximum_fusion, s32[]{:T(128)S(6)} %select_n.48, s32[]{:T(128)S(6)} %select_n.51, ...), kind=kLoop, calls=%fused_computation.77 | loop fusion | bytes 3096592 | tf_op jit(solution)/shard_map/dynamic_slice | solution.py:37
  60.0 2.4 %fusion.23 = (bf16[3,6,4,2688]{3,2,1,0:T(4,128)(2,1)}, bf16[3,6,4,2688]{3,2,1,0:T(4,128)(2,1)}) fusion(s32[]{:T(128)S(6)} %select_n.63, bf16[3,6,4,2688]{3,2,1,0:T(4,128)(2,1)S(1)} %get-tuple-element.13, s32[]{:T(128)S(6)} %select_n.61, bf16[3,6,4,2688]{3,2,1,0:T(4,128)(2,1)S(1)} %get-tuple-element.10), kind=kLoop, calls=%fused_computation.54 | loop fusion | flops 1548288 | bytes 1548296 | tf_op jit(solution)/shard_map/jit(_roll_dynamic)/concatenate | solution.py:38
  62.4 1.2 %reshape.167 = bf16[3,6,4,21,128]{4,3,2,1,0:T(8,128)(2,1)S(1)} reshape(bf16[3,6,4,2688]{3,2,1,0:T(4,128)(2,1)} %get-tuple-element.30) | data formatting | bytes 774144 | tf_op jit(solution)/shard_map/reshape | solution.py:39
  63.6 1.9 %convolution_bitcast_fusion.6 = f32[3,4,21,128]{3,2,1,0:T(8,128)} fusion(bf16[3,6,4,21,128]{4,3,2,1,0:T(8,128)(2,1)S(1)} %reshape.167, bf16[4,3,128,128]{3,2,0,1:T(8,128)(2,1)} %get-tuple-element.34), kind=kOutput, calls=%fused_computation.21 | convolution fusion | flops 33030144 | bytes 647168 | tf_op jit(solution)/shard_map/flsbj,sji->flbi/dot_general | solution.py:45
  65.5 1.8 %convolution_bitcast_fusion.7 = f32[3,4,21,128]{3,2,1,0:T(8,128)} fusion(bf16[3,6,4,21,128]{4,3,2,1,0:T(8,128)(2,1)S(1)} %reshape.167, bf16[4,3,128,128]{3,2,0,1:T(8,128)(2,1)} %get-tuple-element.34), kind=kOutput, calls=%fused_computation.22 | convolution fusion | flops 33030144 | bytes 647168 | tf_op jit(solution)/shard_map/flsbj,sji->flbi/dot_general | solution.py:45
  67.4 1.1 %reshape.166 = bf16[3,6,4,21,128]{4,3,2,1,0:T(8,128)(2,1)S(1)} reshape(bf16[3,6,4,2688]{3,2,1,0:T(4,128)(2,1)} %get-tuple-element.31) | data formatting | bytes 774144 | tf_op jit(solution)/shard_map/reshape | solution.py:39
  68.5 0.0 copy-start.7
  68.5 0.0 copy-start.8
  68.5 0.0 copy-done.6
  68.5 0.9 convolution_bitcast_fusion.9
  69.4 0.9 convolution_bitcast_fusion.10
  70.3 0.0 copy-done.8
  70.4 2.4 %fusion.21 = (bf16[3,6,4,2688]{3,2,1,0:T(4,128)(2,1)}, bf16[3,6,4,2688]{3,2,1,0:T(4,128)(2,1)}) fusion(s32[]{:T(128)S(6)} %select_n.67, bf16[3,6,4,2688]{3,2,1,0:T(4,128)(2,1)S(1)} %copy-done.7, s32[]{:T(128)S(6)} %select_n.65, bf16[3,6,4,2688]{3,2,1,0:T(4,128)(2,1)S(1)} %copy-done.8), kind=kLoop, calls=%fused_computation.52 | loop fusion | flops 1548288 | bytes 1548296 | tf_op jit(solution)/shard_map/jit(_roll_dynamic)/concatenate | solution.py:38
  72.8 1.9 %reshape.169 = bf16[3,6,4,21,128]{4,3,2,1,0:T(8,128)(2,1)} reshape(bf16[3,6,4,2688]{3,2,1,0:T(4,128)(2,1)} %get-tuple-element.28) | data formatting | bytes 774144 | tf_op jit(solution)/shard_map/reshape | solution.py:39
  74.7 1.9 %convolution_bitcast_fusion = f32[3,4,21,128]{3,2,1,0:T(8,128)} fusion(bf16[3,6,4,21,128]{4,3,2,1,0:T(8,128)(2,1)} %reshape.169, bf16[4,3,128,128]{3,2,0,1:T(8,128)(2,1)} %get-tuple-element.32), kind=kOutput, calls=%fused_computation.15 | convolution fusion | flops 33030144 | bytes 702464 | tf_op jit(solution)/shard_map/flsbj,sji->flbi/dot_general | solution.py:45
  76.6 1.9 %convolution_bitcast_fusion.1 = f32[3,4,21,128]{3,2,1,0:T(8,128)} fusion(bf16[3,6,4,21,128]{4,3,2,1,0:T(8,128)(2,1)} %reshape.169, bf16[4,3,128,128]{3,2,0,1:T(8,128)(2,1)} %get-tuple-element.32), kind=kOutput, calls=%fused_computation.16 | convolution fusion | flops 33030144 | bytes 702464 | tf_op jit(solution)/shard_map/flsbj,sji->flbi/dot_general | solution.py:45
  78.5 1.9 %reshape.168 = bf16[3,6,4,21,128]{4,3,2,1,0:T(8,128)(2,1)} reshape(bf16[3,6,4,2688]{3,2,1,0:T(4,128)(2,1)} %get-tuple-element.29) | data formatting | bytes 774144 | tf_op jit(solution)/shard_map/reshape | solution.py:39
  80.4 1.9 %convolution_bitcast_fusion.3 = f32[3,4,21,128]{3,2,1,0:T(8,128)} fusion(bf16[3,6,4,21,128]{4,3,2,1,0:T(8,128)(2,1)} %reshape.168, bf16[4,3,128,128]{3,2,0,1:T(8,128)(2,1)} %get-tuple-element.33), kind=kOutput, calls=%fused_computation.18 | convolution fusion | flops 33030144 | bytes 702464 | tf_op jit(solution)/shard_map/flsbj,sji->flbi/dot_general | solution.py:45
  82.3 1.9 %convolution_bitcast_fusion.4 = f32[3,4,21,128]{3,2,1,0:T(8,128)} fusion(bf16[3,6,4,21,128]{4,3,2,1,0:T(8,128)(2,1)} %reshape.168, bf16[4,3,128,128]{3,2,0,1:T(8,128)(2,1)} %get-tuple-element.33), kind=kOutput, calls=%fused_computation.19 | convolution fusion | flops 33030144 | bytes 702464 | tf_op jit(solution)/shard_map/flsbj,sji->flbi/dot_general | solution.py:45
  84.2 1.9 %fusion.19 = bf16[3,4,21,128]{3,2,1,0:T(8,128)(2,1)} fusion(f32[3,4,21,128]{3,2,1,0:T(8,128)} %convolution_bitcast_fusion.6, f32[3,4,21,128]{3,2,1,0:T(8,128)} %convolution_bitcast_fusion.7, bf16[3,6,4,21,128]{4,3,2,1,0:T(8,128)(2,1)S(1)} %copy-done.3, bf16[4,3,128,128]{3,2,0,1:T(8,128)(2,1)} %get-tuple-element.34), kind=kOutput, calls=%fused_computation.37 | convolution fusion | flops 33126912 | bytes 877568 | tf_op jit(solution)/shard_map/flsbj,sji->flbi/dot_general | solution.py:45
  86.1 1.6 %stack_reshape.17 = bf16[3,4,1,2688]{3,1,0,2:T(4,128)(2,1)} reshape(bf16[3,4,21,128]{3,2,1,0:T(8,128)(2,1)} %fusion.19) | data formatting | bytes 129024 | tf_op jit(solution)/shard_map/stack;reshape | solution.py:64
  87.7 1.9 %fusion.20 = bf16[3,4,21,128]{3,2,1,0:T(8,128)(2,1)} fusion(f32[3,4,21,128]{3,2,1,0:T(8,128)} %convolution_bitcast_fusion.9, f32[3,4,21,128]{3,2,1,0:T(8,128)} %convolution_bitcast_fusion.10, bf16[3,6,4,21,128]{4,3,2,1,0:T(8,128)(2,1)S(1)} %reshape.166, bf16[4,3,128,128]{3,2,0,1:T(8,128)(2,1)S(1)} %copy-done.6), kind=kOutput, calls=%fused_computation.38 | convolution fusion | flops 33126912 | bytes 896000 | tf_op jit(solution)/shard_map/flsbj,sji->flbi/dot_general | solution.py:45
  89.5 0.9 stack_reshape.16
  90.5 1.4 %fusion.17 = bf16[3,4,21,128]{3,2,1,0:T(8,128)(2,1)S(1)} fusion(f32[3,4,21,128]{3,2,1,0:T(8,128)} %convolution_bitcast_fusion, f32[3,4,21,128]{3,2,1,0:T(8,128)} %convolution_bitcast_fusion.1, bf16[3,6,4,21,128]{4,3,2,1,0:T(8,128)(2,1)} %reshape.169, bf16[4,3,128,128]{3,2,0,1:T(8,128)(2,1)} %get-tuple-element.32), kind=kOutput, calls=%fused_computation.35 | convolution fusion | flops 33126912 | bytes 932864 | tf_op jit(solution)/shard_map/flsbj,sji->flbi/dot_general | solution.py:45
  91.9 1.4 %fusion.18 = bf16[3,4,21,128]{3,2,1,0:T(8,128)(2,1)S(1)} fusion(f32[3,4,21,128]{3,2,1,0:T(8,128)} %convolution_bitcast_fusion.3, f32[3,4,21,128]{3,2,1,0:T(8,128)} %convolution_bitcast_fusion.4, bf16[3,6,4,21,128]{4,3,2,1,0:T(8,128)(2,1)} %reshape.168, bf16[4,3,128,128]{3,2,0,1:T(8,128)(2,1)} %get-tuple-element.33), kind=kOutput, calls=%fused_computation.36 | convolution fusion | flops 33126912 | bytes 932864 | tf_op jit(solution)/shard_map/flsbj,sji->flbi/dot_general | solution.py:45
  93.4 0.2 pad_maximum_fusion.4
  93.6 0.1 copy.56
  93.7 0.1 convert_element_type.46
  93.8 0.5 convolution_convert_fusion
  94.3 0.2 copy.58
  94.6 1.0 reshape.198
  95.6 3.5 %all-to-all-start = ((bf16[4,2,1536]{2,1,0:T(2,128)(2,1)}), bf16[4,2,1536]{2,1,0:T(2,128)(2,1)S(1)}, u32[]{:S(2)}, u32[]{:S(2)}) async-start(bf16[4,2,1536]{2,1,0:T(2,128)(2,1)} %reshape.198), calls=%async_computation | async-start | bytes 49152 | tf_op jit(solution)/shard_map/all_to_all | solution.py:75
  99.1 0.1 iota_compare_fusion
  99.2 3.6 %all-to-all-done = bf16[4,2,1536]{2,1,0:T(2,128)(2,1)S(1)} async-done(((bf16[4,2,1536]{2,1,0:T(2,128)(2,1)}), bf16[4,2,1536]{2,1,0:T(2,128)(2,1)S(1)}, u32[]{:S(2)}, u32[]{:S(2)}) %all-to-all-start) | async-done | bytes 24608 | tf_op jit(solution)/shard_map/all_to_all | solution.py:75
  102.8 0.6 reshape.199
  103.5 1.1 %fusion = bf16[12,32,2,1280]{3,0,2,1:T(8,128)(2,1)S(1)} fusion(pred[32,1280]{1,0:T(8,128)(4,1)S(1)} %iota_compare_fusion, bf16[32,16,1280]{2,1,0:T(8,128)(2,1)S(1)} %copy-done, bf16[12,16,32,2]{0,3,2,1:T(2,128)(2,1)S(1)} %bitcast.196), kind=kOutput, calls=%fused_computation.1 | convolution fusion | flops 33423360 | bytes 3342336 | tf_op jit(solution)/shard_map/arqc,qrn->aqcn/dot_general | solution.py:77
  104.6 1.1 copy.62
  105.7 3.3 %copy.63 = bf16[3,4,32,2,1280]{4,3,2,1,0:T(2,128)(2,1)} copy(bf16[3,4,32,2,1280]{4,2,3,1,0:T(8,128)(2,1)S(1)} %bitcast.195) | data formatting | bytes 3932160 | tf_op jit(solution)/shard_map/reshape | solution.py:80
  (19 shorter events, 0.2 us)
Async XLA Ops:
  0.0 103.5 %copy-start = (bf16[32,16,1280]{2,1,0:T(8,128)(2,1)S(1)}, bf16[32,16,1280]{2,1,0:T(8,128)(2,1)}, u32[]{:S(2)}) copy-start(bf16[32,16,1280]{2,1,0:T(8,128)(2,1)} %param.13) | copy-start | bytes 3932164
  2.2 15.3 %copy-start.11 = (s32[128]{0:T(128)S(1)}, s32[128]{0:T(128)}, u32[]{:S(2)}) copy-start(s32[128]{0:T(128)} %param.12) | copy-start | bytes 1540
  2.2 15.4 %copy-start.10 = (s32[4]{0:T(128)S(1)}, s32[4]{0:T(128)}, u32[]{:S(2)}) copy-start(s32[4]{0:T(128)} %param.9) | copy-start | bytes 52
  2.2 35.5 %collective-permute-start = (bf16[3,4,3,2688]{3,2,1,0:T(4,128)(2,1)}, bf16[3,4,3,2688]{3,2,1,0:T(4,128)(2,1)}, u32[]{:S(2)}, u32[]{:S(2)}) collective-permute-start(bf16[3,4,3,2688]{3,2,1,0:T(4,128)(2,1)} %get-tuple-element.16), channel_id=1, source_target_pairs={{0,8},{8,16},{16,24},{1,9},{9,17},{17,25},{2,10},{10,18},{18,26},{... | collective-permute-start | bytes 580616 | tf_op jit(solution)/shard_map/ppermute | solution.py:17
  4.8 32.9 %collective-permute-start.1 = (bf16[3,4,3,2688]{3,2,1,0:T(4,128)(2,1)}, bf16[3,4,3,2688]{3,2,1,0:T(4,128)(2,1)}, u32[]{:S(2)}, u32[]{:S(2)}) collective-permute-start(bf16[3,4,3,2688]{3,2,1,0:T(4,128)(2,1)} %get-tuple-element.17), channel_id=1, source_target_pairs={{8,0},{16,8},{24,16},{9,1},{17,9},{25,17},{10,2},{18,10},{26,18},{... | collective-permute-start | bytes 580616 | tf_op jit(solution)/shard_map/ppermute | solution.py:20
  23.5 2.5 %copy-start.1 = (f32[2688,128,1]{1,0,2:T(8,128)S(1)}, f32[2688,128,1]{1,0,2:T(8,128)}, u32[]{:S(2)}) copy-start(f32[2688,128,1]{1,0,2:T(8,128)} %get-tuple-element.19) | copy-start | bytes 4128772
  32.2 5.5 %copy-start.4 = (bf16[3,4,4,2688]{3,2,1,0:T(4,128)(2,1)S(1)}, bf16[3,4,4,2688]{3,2,1,0:T(4,128)(2,1)}, u32[]{:S(2)}) copy-start(bf16[3,4,4,2688]{3,2,1,0:T(4,128)(2,1)} %param.8) | copy-start | bytes 774148
  35.6 10.3 %copy-start.5 = (bf16[1,4,3,128,128]{4,3,2,1,0:T(8,128)(2,1)S(1)}, bf16[1,4,3,128,128]{4,3,2,1,0:T(8,128)(2,1)}, u32[]{:S(2)}) copy-start(bf16[1,4,3,128,128]{4,3,2,1,0:T(8,128)(2,1)} %get-tuple-element.9) | copy-start | bytes 1179652
  38.9 14.7 %collective-permute-start.2 = (bf16[3,1,10,2688]{3,2,1,0:T(8,128)(2,1)S(1)}, bf16[3,1,10,2688]{3,2,1,0:T(8,128)(2,1)S(1)}, u32[]{:S(2)}, u32[]{:S(2)}) collective-permute-start(bf16[3,1,10,2688]{3,2,1,0:T(8,128)(2,1)S(1)} %get-tuple-element.14), channel_id=1, source_target_pairs={{0,1},{1,2},{2,3},{3,4},{4,5},{5,6},{6,7},{8,9},{9,10},{10,11},{11... | collective-permute-start | bytes 483848 | tf_op jit(solution)/shard_map/ppermute | solution.py:17
  42.4 13.9 %collective-permute-start.3 = (bf16[3,1,10,2688]{3,2,1,0:T(8,128)(2,1)S(1)}, bf16[3,1,10,2688]{3,2,1,0:T(8,128)(2,1)S(1)}, u32[]{:S(2)}, u32[]{:S(2)}) collective-permute-start(bf16[3,1,10,2688]{3,2,1,0:T(8,128)(2,1)S(1)} %get-tuple-element.15), channel_id=1, source_target_pairs={{1,0},{2,1},{3,2},{4,3},{5,4},{6,5},{7,6},{9,8},{10,9},{11,10},{12... | collective-permute-start | bytes 483848 | tf_op jit(solution)/shard_map/ppermute | solution.py:20
  62.4 6.1 %copy-start.6 = (bf16[4,3,128,128]{3,2,0,1:T(8,128)(2,1)S(1)}, bf16[4,3,128,128]{3,2,0,1:T(8,128)(2,1)}, u32[]{:S(2)}) copy-start(bf16[4,3,128,128]{3,2,0,1:T(8,128)(2,1)} %get-tuple-element.35) | copy-start | bytes 1179652
  63.6 3.8 %copy-start.2 = (bf16[3,6,4,21,128]{4,3,2,1,0:T(8,128)(2,1)}, bf16[3,6,4,21,128]{4,3,2,1,0:T(8,128)(2,1)S(1)}, u32[]{:S(2)}) copy-start(bf16[3,6,4,21,128]{4,3,2,1,0:T(8,128)(2,1)S(1)} %reshape.167) | copy-start | bytes 1161220
  68.5 1.8 %copy-start.7 = (bf16[3,6,4,2688]{3,2,1,0:T(4,128)(2,1)S(1)}, bf16[3,6,4,2688]{3,2,1,0:T(4,128)(2,1)}, u32[]{:S(2)}) copy-start(bf16[3,6,4,2688]{3,2,1,0:T(4,128)(2,1)} %get-tuple-element.11) | copy-start | bytes 1161220
  68.5 1.8 %copy-start.8 = (bf16[3,6,4,2688]{3,2,1,0:T(4,128)(2,1)S(1)}, bf16[3,6,4,2688]{3,2,1,0:T(4,128)(2,1)}, u32[]{:S(2)}) copy-start(bf16[3,6,4,2688]{3,2,1,0:T(4,128)(2,1)} %get-tuple-element.12) | copy-start | bytes 1161220
  80.4 3.8 %copy-start.3 = (bf16[3,6,4,21,128]{4,3,2,1,0:T(8,128)(2,1)S(1)}, bf16[3,6,4,21,128]{4,3,2,1,0:T(8,128)(2,1)}, u32[]{:S(2)}) copy-start(bf16[3,6,4,21,128]{4,3,2,1,0:T(8,128)(2,1)} %copy-done.2) | copy-start | bytes 1161220
  89.5 3.8 %copy-start.9 = (bf16[3,4,1,2688]{3,1,0,2:T(4,128)(2,1)S(1)}, bf16[3,4,1,2688]{3,1,0,2:T(4,128)(2,1)}, u32[]{:S(2)}) copy-start(bf16[3,4,1,2688]{3,1,0,2:T(4,128)(2,1)} %stack_reshape.17) | copy-start | bytes 193540
  95.6 7.2 %all-to-all-start = ((bf16[4,2,1536]{2,1,0:T(2,128)(2,1)}), bf16[4,2,1536]{2,1,0:T(2,128)(2,1)S(1)}, u32[]{:S(2)}, u32[]{:S(2)}) async-start(bf16[4,2,1536]{2,1,0:T(2,128)(2,1)} %reshape.198), calls=%async_computation | async-start | bytes 49152 | tf_op jit(solution)/shard_map/all_to_all | solution.py:75
where the time goes:
time: 110 us; the launch traced here: 109 us
  local copies, waits for them, and re-layouts  35.3 us (32%)
  matrix products  21.3 us (19%)
  other arithmetic  16.8 us (15%)
  starting transfers between devices  14.3 us (13%)
  waiting for transfers between devices  13 us (12%)
  between operations  8.25 us (8%)
    dot_general x12, matrix products, vertical_terms(): jnp.einsum('flsbj,sji->flbi', rows[:, level_step:level_step + depth], wei...  19.7 us
    convert_element_type x2, local copies, waits for them, and re-layouts, make_table(): (paired.reshape(longitudes, 2 * waves.shape[0]) / math.sqrt(longitudes))....  8.07 us
    cos x1, other arithmetic, make_table(): paired = jnp.stack([jnp.cos(angle), -jnp.sin(angle)], axis=2)  7.3 us
    ppermute x2, waiting for transfers between devices, with_halo(): lax.ppermute(lax.slice_in_dim(block, block.shape[dim] - width, None, axis...  6.76 us
    reshape x4, local copies, waits for them, and re-layouts, stencil_rows(): rows.reshape(rows.shape[0], rows.shape[1], STENCIL, rows.shape[3] // BLK,...  6.17 us
    ppermute x2, starting transfers between devices, with_halo(): lax.ppermute(lax.slice_in_dim(block, block.shape[dim] - width, None, axis...  6 us
    concatenate x2, other arithmetic, stencil_rows(): rows = jnp.roll(rows, -block_shift[row_index] * BLK, axis=3)  4.86 us
    ppermute x2, starting transfers between devices, with_halo(): lax.ppermute(lax.slice_in_dim(block, 0, width, axis=dim), axis, backward)  4.77 us
  transfers between devices with their start and end apart: 5, of which 3 were waited for; matrix products, arithmetic and copies ran while one was open for 23% of the time, Pallas kernels for 0%

commit v1 on v0

--- a/solution.py
+++ b/solution.py
@@ -72,7 +72,10 @@
         interp.reshape(items * lat_rows, longitudes), table, preferred_element_type=jnp.float32
     )
     fourier = fourier.astype(jnp.bfloat16).reshape(items, lat_rows, table.shape[1])
-    coeffs = lax.all_to_all(fourier, "band", split_axis=2, concat_axis=1, tiled=True)
+    coeffs = jnp.concatenate(
+        lax.all_to_all(jnp.stack(jnp.split(fourier, lax.axis_size("band"), axis=2)), "band", 0, 0),
+        axis=1,
+    )
     shaped = coeffs.reshape(coeffs.shape[0], latitudes, owned, 2)
     result = jnp.einsum("arqc,qrn->aqcn", shaped, legendre, preferred_element_type=jnp.float32)
     result = jnp.where(keep[None, :, None, :], result, jnp.zeros((), jnp.float32))

time: 110 us -> 109 us (level)
  no operation moved by 1% of the time
where the time goes in v1:
time: 109 us; the launch traced here: 108 us
  local copies, waits for them, and re-layouts  34.5 us (32%)
  matrix products  21.3 us (20%)
  other arithmetic  16.8 us (15%)
  starting transfers between devices  14.3 us (13%)
  waiting for transfers between devices  13.1 us (12%)
  between operations  8 us (7%)
    dot_general x12, matrix products, vertical_terms(): jnp.einsum('flsbj,sji->flbi', rows[:, level_step:level_step + depth], wei...  19.7 us
    convert_element_type x2, local copies, waits for them, and re-layouts, make_table(): (paired.reshape(longitudes, 2 * waves.shape[0]) / math.sqrt(longitudes))....  8.06 us
    cos x1, other arithmetic, make_table(): paired = jnp.stack([jnp.cos(angle), -jnp.sin(angle)], axis=2)  7.3 us
    ppermute x2, waiting for transfers between devices, with_halo(): lax.ppermute(lax.slice_in_dim(block, block.shape[dim] - width, None, axis...  6.77 us
    reshape x4, local copies, waits for them, and re-layouts, stencil_rows(): rows.reshape(rows.shape[0], rows.shape[1], STENCIL, rows.shape[3] // BLK,...  6.16 us
    ppermute x2, starting transfers between devices, with_halo(): lax.ppermute(lax.slice_in_dim(block, block.shape[dim] - width, None, axis...  6 us
    concatenate x2, other arithmetic, stencil_rows(): rows = jnp.roll(rows, -block_shift[row_index] * BLK, axis=3)  4.81 us
    ppermute x2, starting transfers between devices, with_halo(): lax.ppermute(lax.slice_in_dim(block, 0, width, axis=dim), axis, backward)  4.77 us
  transfers between devices with their start and end apart: 5, of which 3 were waited for; matrix products, arithmetic and copies ran while one was open for 23% of the time, Pallas kernels for 0%

profile of v1, /device:TPU:8, one launch (start us, length us, event | category | flops | bytes accessed | tf_op | source)
XLA Modules:
  0.0 107.9 jit_solution(9838268111448065872)
XLA Ops:
  0.0 0.0 copy-start
  0.0 2.2 %fusion.27 = (bf16[3,4,3,2688]{3,2,1,0:T(4,128)(2,1)}, bf16[3,4,3,2688]{3,2,1,0:T(4,128)(2,1)}) fusion(bf16[3,4,4,2688]{3,2,1,0:T(4,128)(2,1)} %param.8), kind=kLoop, calls=%fused_computation.84 | loop fusion | bytes 774144 | tf_op jit(solution)/shard_map/slice | solution.py:18
  2.2 2.6 %collective-permute-start = (bf16[3,4,3,2688]{3,2,1,0:T(4,128)(2,1)}, bf16[3,4,3,2688]{3,2,1,0:T(4,128)(2,1)}, u32[]{:S(2)}, u32[]{:S(2)}) collective-permute-start(bf16[3,4,3,2688]{3,2,1,0:T(4,128)(2,1)} %get-tuple-element.16), channel_id=1, source_target_pairs={{0,8},{8,16},{16,24},{1,9},{9,17},{17,25},{2,10},{10,18},{18,26},{... | collective-permute-start | bytes 580616 | tf_op jit(solution)/shard_map/ppermute | solution.py:17
  4.8 1.3 %collective-permute-start.1 = (bf16[3,4,3,2688]{3,2,1,0:T(4,128)(2,1)}, bf16[3,4,3,2688]{3,2,1,0:T(4,128)(2,1)}, u32[]{:S(2)}, u32[]{:S(2)}) collective-permute-start(bf16[3,4,3,2688]{3,2,1,0:T(4,128)(2,1)} %get-tuple-element.17), channel_id=1, source_target_pairs={{8,0},{16,8},{24,16},{9,1},{17,9},{25,17},{10,2},{18,10},{26,18},{... | collective-permute-start | bytes 580616 | tf_op jit(solution)/shard_map/ppermute | solution.py:20
  6.1 1.5 %fusion.29 = (s32[1]{0:T(128)}, s32[1]{0:T(128)}, s32[1]{0:T(128)}, s32[1]{0:T(128)}) fusion(s32[4]{0:T(128)} %param.10), kind=kLoop, calls=%fused_computation.86 | loop fusion | bytes 32 | tf_op jit(solution)/shard_map/slice | solution.py:38
  10.2 7.3 %fusion.6 = (f32[2688,128,1]{1,0,2:T(8,128)S(1)}, f32[2688,128,1]{1,0,2:T(8,128)}) fusion(s32[128]{0:T(128)} %param.12), kind=kLoop, calls=%fused_computation.12 | loop fusion | flops 3440640 | bytes 2753024 | tf_op jit(solution)/shard_map/cos | solution.py:29
  17.5 0.0 copy-done.11
  17.5 0.1 dynamic_slice.18
  17.6 0.0 copy-done.10
  17.6 0.7 fusion.28
  23.3 0.0 copy-start.1
  23.3 2.5 %fusion.26 = (bf16[1,4,3,128,128]{4,3,2,1,0:T(8,128)(2,1)}, bf16[1,4,3,128,128]{4,3,2,1,0:T(8,128)(2,1)S(1)}, bf16[1,4,3,128,128]{4,3,2,1,0:T(8,128)(2,1)}, bf16[1,4,3,128,128]{4,3,2,1,0:T(8,128)(2,1)}) fusion(bf16[4,4,3,128,128]{4,3,2,1,0:T(8,128)(2,1)} %param.11), kind=kLoop, calls=%fused_computation.83 | loop fusion | bytes 3145728 | tf_op jit(solution)/shard_map/slice | solution.py:63
  25.8 1.4 %fusion.1 = bf16[2688,128,2]{1,0,2:T(8,128)(2,1)} fusion(f32[2688,128,1]{1,0,2:T(8,128)S(1)} %copy-done.1, f32[2688,128,1]{1,0,2:T(8,128)S(1)} %get-tuple-element.22), kind=kLoop, calls=%fused_computation.3 | loop fusion | flops 2064384 | bytes 4128768 | tf_op jit(solution)/shard_map/convert_element_type | solution.py:30
  27.2 4.8 %copy.39 = bf16[2688,128,2]{0,2,1:T(2,128)(2,1)} copy(bf16[2688,128,2]{1,0,2:T(8,128)(2,1)} %fusion.1) | data formatting | bytes 2752512 | tf_op jit(solution)/shard_map/convert_element_type | solution.py:30
  32.0 3.3 %convert_element_type.49 = bf16[2688,256]{0,1:T(8,128)(2,1)S(1)} reshape(bf16[2688,128,2]{0,2,1:T(2,128)(2,1)} %copy.39) | data formatting | bytes 2752512 | tf_op jit(solution)/shard_map/convert_element_type | solution.py:30
  35.3 2.1 %copy_bitcast_fusion.2 = (bf16[4,3,128,128]{3,2,0,1:T(8,128)(2,1)}, bf16[4,3,128,128]{3,2,0,1:T(8,128)(2,1)}) fusion(bf16[1,4,3,128,128]{4,3,2,1,0:T(8,128)(2,1)} %get-tuple-element.8, bf16[1,4,3,128,128]{4,3,2,1,0:T(8,128)(2,1)} %get-tuple-element.6), kind=kLoop, calls=%fused_computation.50 | loop fusion | bytes 1572864 | tf_op jit(solution)/shard_map/squeeze | solution.py:63
  37.5 0.0 collective-permute-done
  37.5 0.0 collective-permute-done.1
  37.5 0.0 copy-done.4
  37.5 1.2 %pad_maximum_fusion.3 = (bf16[3,1,10,2688]{3,2,1,0:T(8,128)(2,1)S(1)}, bf16[3,1,10,2688]{3,2,1,0:T(8,128)(2,1)S(1)}) fusion(bf16[3,4,3,2688]{3,2,1,0:T(4,128)(2,1)} %collective-permute-done.1, bf16[3,4,4,2688]{3,2,1,0:T(4,128)(2,1)S(1)} %copy-done.4, bf16[3,4,3,2688]{3,2,1,0:T(4,128)(2,1)} %collective-permute-done), kind=kLoop, calls=%fused_computation.59 | loop fusion | flops 967680 | bytes 967680 | tf_op jit(solution)/shard_map/slice | solution.py:18
  38.7 3.4 %collective-permute-start.2 = (bf16[3,1,10,2688]{3,2,1,0:T(8,128)(2,1)S(1)}, bf16[3,1,10,2688]{3,2,1,0:T(8,128)(2,1)S(1)}, u32[]{:S(2)}, u32[]{:S(2)}) collective-permute-start(bf16[3,1,10,2688]{3,2,1,0:T(8,128)(2,1)S(1)} %get-tuple-element.14), channel_id=1, source_target_pairs={{0,1},{1,2},{2,3},{3,4},{4,5},{5,6},{6,7},{8,9},{9,10},{10,11},{11... | collective-permute-start | bytes 483848 | tf_op jit(solution)/shard_map/ppermute | solution.py:17
  42.1 3.5 %collective-permute-start.3 = (bf16[3,1,10,2688]{3,2,1,0:T(8,128)(2,1)S(1)}, bf16[3,1,10,2688]{3,2,1,0:T(8,128)(2,1)S(1)}, u32[]{:S(2)}, u32[]{:S(2)}) collective-permute-start(bf16[3,1,10,2688]{3,2,1,0:T(8,128)(2,1)S(1)} %get-tuple-element.15), channel_id=1, source_target_pairs={{1,0},{2,1},{3,2},{4,3},{5,4},{6,5},{7,6},{9,8},{10,9},{11,10},{12... | collective-permute-start | bytes 483848 | tf_op jit(solution)/shard_map/ppermute | solution.py:20
  45.7 1.0 copy_bitcast_fusion
  46.6 6.8 %collective-permute-done.2 = bf16[3,1,10,2688]{3,2,1,0:T(8,128)(2,1)S(1)} collective-permute-done((bf16[3,1,10,2688]{3,2,1,0:T(8,128)(2,1)S(1)}, bf16[3,1,10,2688]{3,2,1,0:T(8,128)(2,1)S(1)}, u32[]{:S(2)}, u32[]{:S(2)}) %collective-permute-start.2) | collective-permute-done | bytes 161312 | tf_op jit(solution)/shard_map/ppermute | solution.py:17
  53.4 2.7 %collective-permute-done.3 = bf16[3,1,10,2688]{3,2,1,0:T(8,128)(2,1)S(1)} collective-permute-done((bf16[3,1,10,2688]{3,2,1,0:T(8,128)(2,1)S(1)}, bf16[3,1,10,2688]{3,2,1,0:T(8,128)(2,1)S(1)}, u32[]{:S(2)}, u32[]{:S(2)}) %collective-permute-start.3) | collective-permute-done | bytes 161312 | tf_op jit(solution)/shard_map/ppermute | solution.py:20
  56.1 1.7 %pad_maximum_fusion = bf16[3,6,10,2688]{3,2,1,0:T(8,128)(2,1)S(1)} fusion(bf16[3,1,10,2688]{3,2,1,0:T(8,128)(2,1)S(1)} %collective-permute-done.3, bf16[3,4,3,2688]{3,2,1,0:T(4,128)(2,1)} %collective-permute-done.1, bf16[3,4,4,2688]{3,2,1,0:T(4,128)(2,1)S(1)} %copy-done.4, bf16[3,4,3,2688]{3,2,1,0:T(4,128)(2,1)} %collective-permute-done, ...), kind=kLoop, calls=%fused_computation.5 | loop fusion | flops 4838400 | bytes 1935360 | tf_op jit(solution)/shard_map/concatenate | solution.py:21
  57.8 1.9 %constant_dynamic-slice_fusion.3 = (bf16[3,6,4,2688]{3,2,1,0:T(4,128)(2,1)S(1)}, bf16[3,6,4,2688]{3,2,1,0:T(4,128)(2,1)}, bf16[3,6,4,2688]{3,2,1,0:T(4,128)(2,1)}, bf16[3,6,4,2688]{3,2,1,0:T(4,128)(2,1)S(1)}) fusion(bf16[3,6,10,2688]{3,2,1,0:T(8,128)(2,1)S(1)} %pad_maximum_fusion, s32[]{:T(128)S(6)} %select_n.48, s32[]{:T(128)S(6)} %select_n.51, ...), kind=kLoop, calls=%fused_computation.82 | loop fusion | bytes 3096592 | tf_op jit(solution)/shard_map/dynamic_slice | solution.py:37
  59.7 2.4 %fusion.23 = (bf16[3,6,4,2688]{3,2,1,0:T(4,128)(2,1)}, bf16[3,6,4,2688]{3,2,1,0:T(4,128)(2,1)}) fusion(s32[]{:T(128)S(6)} %select_n.63, bf16[3,6,4,2688]{3,2,1,0:T(4,128)(2,1)S(1)} %get-tuple-element.13, s32[]{:T(128)S(6)} %select_n.61, bf16[3,6,4,2688]{3,2,1,0:T(4,128)(2,1)S(1)} %get-tuple-element.10), kind=kLoop, calls=%fused_computation.54 | loop fusion | flops 1548288 | bytes 1548296 | tf_op jit(solution)/shard_map/jit(_roll_dynamic)/concatenate | solution.py:38
  62.1 1.2 %reshape.166 = bf16[3,6,4,21,128]{4,3,2,1,0:T(8,128)(2,1)S(1)} reshape(bf16[3,6,4,2688]{3,2,1,0:T(4,128)(2,1)} %get-tuple-element.34) | data formatting | bytes 774144 | tf_op jit(solution)/shard_map/reshape | solution.py:39
  63.3 0.0 copy-start.2
  63.3 1.9 %convolution_bitcast_fusion.6 = f32[3,4,21,128]{3,2,1,0:T(8,128)} fusion(bf16[3,6,4,21,128]{4,3,2,1,0:T(8,128)(2,1)S(1)} %reshape.166, bf16[4,3,128,128]{3,2,0,1:T(8,128)(2,1)} %get-tuple-element.38), kind=kOutput, calls=%fused_computation.21 | convolution fusion | flops 33030144 | bytes 647168 | tf_op jit(solution)/shard_map/flsbj,sji->flbi/dot_general | solution.py:45
  65.3 1.8 %convolution_bitcast_fusion.7 = f32[3,4,21,128]{3,2,1,0:T(8,128)} fusion(bf16[3,6,4,21,128]{4,3,2,1,0:T(8,128)(2,1)S(1)} %reshape.166, bf16[4,3,128,128]{3,2,0,1:T(8,128)(2,1)} %get-tuple-element.38), kind=kOutput, calls=%fused_computation.22 | convolution fusion | flops 33030144 | bytes 647168 | tf_op jit(solution)/shard_map/flsbj,sji->flbi/dot_general | solution.py:45
  67.1 1.1 %reshape.165 = bf16[3,6,4,21,128]{4,3,2,1,0:T(8,128)(2,1)S(1)} reshape(bf16[3,6,4,2688]{3,2,1,0:T(4,128)(2,1)} %get-tuple-element.35) | data formatting | bytes 774144 | tf_op jit(solution)/shard_map/reshape | solution.py:39
  68.2 0.9 convolution_bitcast_fusion.9
  69.1 0.9 convolution_bitcast_fusion.10
  70.1 0.0 copy-done.7
  70.1 2.4 %fusion.21 = (bf16[3,6,4,2688]{3,2,1,0:T(4,128)(2,1)}, bf16[3,6,4,2688]{3,2,1,0:T(4,128)(2,1)}) fusion(s32[]{:T(128)S(6)} %select_n.67, bf16[3,6,4,2688]{3,2,1,0:T(4,128)(2,1)S(1)} %copy-done.7, s32[]{:T(128)S(6)} %select_n.65, bf16[3,6,4,2688]{3,2,1,0:T(4,128)(2,1)S(1)} %copy-done.8), kind=kLoop, calls=%fused_computation.52 | loop fusion | flops 1548288 | bytes 1548296 | tf_op jit(solution)/shard_map/jit(_roll_dynamic)/concatenate | solution.py:38
  72.5 1.9 %reshape.168 = bf16[3,6,4,21,128]{4,3,2,1,0:T(8,128)(2,1)} reshape(bf16[3,6,4,2688]{3,2,1,0:T(4,128)(2,1)} %get-tuple-element.32) | data formatting | bytes 774144 | tf_op jit(solution)/shard_map/reshape | solution.py:39
  74.4 1.9 %convolution_bitcast_fusion = f32[3,4,21,128]{3,2,1,0:T(8,128)} fusion(bf16[3,6,4,21,128]{4,3,2,1,0:T(8,128)(2,1)} %reshape.168, bf16[4,3,128,128]{3,2,0,1:T(8,128)(2,1)} %get-tuple-element.36), kind=kOutput, calls=%fused_computation.15 | convolution fusion | flops 33030144 | bytes 702464 | tf_op jit(solution)/shard_map/flsbj,sji->flbi/dot_general | solution.py:45
  76.2 1.9 %convolution_bitcast_fusion.1 = f32[3,4,21,128]{3,2,1,0:T(8,128)} fusion(bf16[3,6,4,21,128]{4,3,2,1,0:T(8,128)(2,1)} %reshape.168, bf16[4,3,128,128]{3,2,0,1:T(8,128)(2,1)} %get-tuple-element.36), kind=kOutput, calls=%fused_computation.16 | convolution fusion | flops 33030144 | bytes 702464 | tf_op jit(solution)/shard_map/flsbj,sji->flbi/dot_general | solution.py:45
  78.2 1.9 %reshape.167 = bf16[3,6,4,21,128]{4,3,2,1,0:T(8,128)(2,1)} reshape(bf16[3,6,4,2688]{3,2,1,0:T(4,128)(2,1)} %get-tuple-element.33) | data formatting | bytes 774144 | tf_op jit(solution)/shard_map/reshape | solution.py:39
  80.1 1.9 %convolution_bitcast_fusion.3 = f32[3,4,21,128]{3,2,1,0:T(8,128)} fusion(bf16[3,6,4,21,128]{4,3,2,1,0:T(8,128)(2,1)} %reshape.167, bf16[4,3,128,128]{3,2,0,1:T(8,128)(2,1)} %get-tuple-element.37), kind=kOutput, calls=%fused_computation.18 | convolution fusion | flops 33030144 | bytes 702464 | tf_op jit(solution)/shard_map/flsbj,sji->flbi/dot_general | solution.py:45
  82.0 1.9 %convolution_bitcast_fusion.4 = f32[3,4,21,128]{3,2,1,0:T(8,128)} fusion(bf16[3,6,4,21,128]{4,3,2,1,0:T(8,128)(2,1)} %reshape.167, bf16[4,3,128,128]{3,2,0,1:T(8,128)(2,1)} %get-tuple-element.37), kind=kOutput, calls=%fused_computation.19 | convolution fusion | flops 33030144 | bytes 702464 | tf_op jit(solution)/shard_map/flsbj,sji->flbi/dot_general | solution.py:45
  83.9 1.9 %fusion.19 = bf16[3,4,21,128]{3,2,1,0:T(8,128)(2,1)} fusion(f32[3,4,21,128]{3,2,1,0:T(8,128)} %convolution_bitcast_fusion.6, f32[3,4,21,128]{3,2,1,0:T(8,128)} %convolution_bitcast_fusion.7, bf16[3,6,4,21,128]{4,3,2,1,0:T(8,128)(2,1)S(1)} %copy-done.3, bf16[4,3,128,128]{3,2,0,1:T(8,128)(2,1)} %get-tuple-element.38), kind=kOutput, calls=%fused_computation.37 | convolution fusion | flops 33126912 | bytes 877568 | tf_op jit(solution)/shard_map/flsbj,sji->flbi/dot_general | solution.py:45
  85.8 1.5 %stack_reshape.17 = bf16[3,4,1,2688]{3,1,0,2:T(4,128)(2,1)} reshape(bf16[3,4,21,128]{3,2,1,0:T(8,128)(2,1)} %fusion.19) | data formatting | bytes 129024 | tf_op jit(solution)/shard_map/stack;reshape | solution.py:64
  87.4 1.8 %fusion.20 = bf16[3,4,21,128]{3,2,1,0:T(8,128)(2,1)} fusion(f32[3,4,21,128]{3,2,1,0:T(8,128)} %convolution_bitcast_fusion.9, f32[3,4,21,128]{3,2,1,0:T(8,128)} %convolution_bitcast_fusion.10, bf16[3,6,4,21,128]{4,3,2,1,0:T(8,128)(2,1)S(1)} %reshape.165, bf16[4,3,128,128]{3,2,0,1:T(8,128)(2,1)S(1)} %copy-done.6), kind=kOutput, calls=%fused_computation.38 | convolution fusion | flops 33126912 | bytes 896000 | tf_op jit(solution)/shard_map/flsbj,sji->flbi/dot_general | solution.py:45
  89.2 0.9 stack_reshape.16
  90.1 1.4 %fusion.17 = bf16[3,4,21,128]{3,2,1,0:T(8,128)(2,1)S(1)} fusion(f32[3,4,21,128]{3,2,1,0:T(8,128)} %convolution_bitcast_fusion, f32[3,4,21,128]{3,2,1,0:T(8,128)} %convolution_bitcast_fusion.1, bf16[3,6,4,21,128]{4,3,2,1,0:T(8,128)(2,1)} %reshape.168, bf16[4,3,128,128]{3,2,0,1:T(8,128)(2,1)} %get-tuple-element.36), kind=kOutput, calls=%fused_computation.35 | convolution fusion | flops 33126912 | bytes 932864 | tf_op jit(solution)/shard_map/flsbj,sji->flbi/dot_general | solution.py:45
  91.6 1.4 %fusion.18 = bf16[3,4,21,128]{3,2,1,0:T(8,128)(2,1)S(1)} fusion(f32[3,4,21,128]{3,2,1,0:T(8,128)} %convolution_bitcast_fusion.3, f32[3,4,21,128]{3,2,1,0:T(8,128)} %convolution_bitcast_fusion.4, bf16[3,6,4,21,128]{4,3,2,1,0:T(8,128)(2,1)} %reshape.167, bf16[4,3,128,128]{3,2,0,1:T(8,128)(2,1)} %get-tuple-element.37), kind=kOutput, calls=%fused_computation.36 | convolution fusion | flops 33126912 | bytes 932864 | tf_op jit(solution)/shard_map/flsbj,sji->flbi/dot_general | solution.py:45
  93.0 0.2 pad_maximum_fusion.4
  93.3 0.1 copy.38
  93.4 0.1 convert_element_type.46
  93.5 0.5 convolution_convert_fusion
  94.0 0.1 slice_bitcast_fusion.27
  94.1 0.1 pad_maximum_fusion.5
  94.2 0.7 reshape.197
  94.9 3.5 %all-to-all-start = ((bf16[4,2,1536]{2,1,0:T(2,128)(2,1)}), bf16[4,2,1536]{2,1,0:T(2,128)(2,1)S(1)}, u32[]{:S(2)}, u32[]{:S(2)}) async-start(bf16[4,2,1536]{2,1,0:T(2,128)(2,1)} %reshape.197), calls=%async_computation | async-start | bytes 49152 | tf_op jit(solution)/shard_map/all_to_all | solution.py:76
  98.4 0.1 iota_compare_fusion
  98.5 3.6 %all-to-all-done = bf16[4,2,1536]{2,1,0:T(2,128)(2,1)S(1)} async-done(((bf16[4,2,1536]{2,1,0:T(2,128)(2,1)}), bf16[4,2,1536]{2,1,0:T(2,128)(2,1)S(1)}, u32[]{:S(2)}, u32[]{:S(2)}) %all-to-all-start) | async-done | bytes 24608 | tf_op jit(solution)/shard_map/all_to_all | solution.py:76
  102.1 0.1 reshape.198
  102.2 0.2 copy.40
  102.4 1.1 %fusion = bf16[12,32,2,1280]{3,0,2,1:T(8,128)(2,1)S(1)} fusion(pred[32,1280]{1,0:T(8,128)(4,1)S(1)} %iota_compare_fusion, bf16[32,16,1280]{2,1,0:T(8,128)(2,1)S(1)} %copy-done, bf16[12,16,32,2]{0,3,2,1:T(2,128)(2,1)S(1)} %bitcast.199), kind=kOutput, calls=%fused_computation.1 | convolution fusion | flops 33423360 | bytes 3342336 | tf_op jit(solution)/shard_map/arqc,qrn->aqcn/dot_general | solution.py:80
  103.6 1.1 %copy.42 = bf16[12,32,2,1280]{3,1,2,0:T(8,128)(2,1)S(1)} copy(bf16[12,32,2,1280]{3,0,2,1:T(8,128)(2,1)S(1)} %fusion) | data formatting | bytes 3932160 | tf_op jit(solution)/shard_map/convert_element_type | solution.py:82
  104.6 3.3 %copy.43 = bf16[3,4,32,2,1280]{4,3,2,1,0:T(2,128)(2,1)} copy(bf16[3,4,32,2,1280]{4,2,3,1,0:T(8,128)(2,1)S(1)} %bitcast.198) | data formatting | bytes 3932160 | tf_op jit(solution)/shard_map/reshape | solution.py:83
  (20 shorter events, 0.2 us)
Async XLA Ops:
  0.0 102.4 %copy-start = (bf16[32,16,1280]{2,1,0:T(8,128)(2,1)S(1)}, bf16[32,16,1280]{2,1,0:T(8,128)(2,1)}, u32[]{:S(2)}) copy-start(bf16[32,16,1280]{2,1,0:T(8,128)(2,1)} %param.13) | copy-start | bytes 3932164
  2.2 15.3 %copy-start.11 = (s32[128]{0:T(128)S(1)}, s32[128]{0:T(128)}, u32[]{:S(2)}) copy-start(s32[128]{0:T(128)} %param.12) | copy-start | bytes 1540
  2.2 15.4 %copy-start.10 = (s32[4]{0:T(128)S(1)}, s32[4]{0:T(128)}, u32[]{:S(2)}) copy-start(s32[4]{0:T(128)} %param.9) | copy-start | bytes 52
  2.2 35.2 %collective-permute-start = (bf16[3,4,3,2688]{3,2,1,0:T(4,128)(2,1)}, bf16[3,4,3,2688]{3,2,1,0:T(4,128)(2,1)}, u32[]{:S(2)}, u32[]{:S(2)}) collective-permute-start(bf16[3,4,3,2688]{3,2,1,0:T(4,128)(2,1)} %get-tuple-element.16), channel_id=1, source_target_pairs={{0,8},{8,16},{16,24},{1,9},{9,17},{17,25},{2,10},{10,18},{18,26},{... | collective-permute-start | bytes 580616 | tf_op jit(solution)/shard_map/ppermute | solution.py:17
  4.8 32.7 %collective-permute-start.1 = (bf16[3,4,3,2688]{3,2,1,0:T(4,128)(2,1)}, bf16[3,4,3,2688]{3,2,1,0:T(4,128)(2,1)}, u32[]{:S(2)}, u32[]{:S(2)}) collective-permute-start(bf16[3,4,3,2688]{3,2,1,0:T(4,128)(2,1)} %get-tuple-element.17), channel_id=1, source_target_pairs={{8,0},{16,8},{24,16},{9,1},{17,9},{25,17},{10,2},{18,10},{26,18},{... | collective-permute-start | bytes 580616 | tf_op jit(solution)/shard_map/ppermute | solution.py:20
  23.3 2.5 %copy-start.1 = (f32[2688,128,1]{1,0,2:T(8,128)S(1)}, f32[2688,128,1]{1,0,2:T(8,128)}, u32[]{:S(2)}) copy-start(f32[2688,128,1]{1,0,2:T(8,128)} %get-tuple-element.23) | copy-start | bytes 4128772
  32.0 5.5 %copy-start.4 = (bf16[3,4,4,2688]{3,2,1,0:T(4,128)(2,1)S(1)}, bf16[3,4,4,2688]{3,2,1,0:T(4,128)(2,1)}, u32[]{:S(2)}) copy-start(bf16[3,4,4,2688]{3,2,1,0:T(4,128)(2,1)} %param.8) | copy-start | bytes 774148
  35.3 10.3 %copy-start.5 = (bf16[1,4,3,128,128]{4,3,2,1,0:T(8,128)(2,1)S(1)}, bf16[1,4,3,128,128]{4,3,2,1,0:T(8,128)(2,1)}, u32[]{:S(2)}) copy-start(bf16[1,4,3,128,128]{4,3,2,1,0:T(8,128)(2,1)} %get-tuple-element.9) | copy-start | bytes 1179652
  38.7 14.7 %collective-permute-start.2 = (bf16[3,1,10,2688]{3,2,1,0:T(8,128)(2,1)S(1)}, bf16[3,1,10,2688]{3,2,1,0:T(8,128)(2,1)S(1)}, u32[]{:S(2)}, u32[]{:S(2)}) collective-permute-start(bf16[3,1,10,2688]{3,2,1,0:T(8,128)(2,1)S(1)} %get-tuple-element.14), channel_id=1, source_target_pairs={{0,1},{1,2},{2,3},{3,4},{4,5},{5,6},{6,7},{8,9},{9,10},{10,11},{11... | collective-permute-start | bytes 483848 | tf_op jit(solution)/shard_map/ppermute | solution.py:17
  42.1 13.9 %collective-permute-start.3 = (bf16[3,1,10,2688]{3,2,1,0:T(8,128)(2,1)S(1)}, bf16[3,1,10,2688]{3,2,1,0:T(8,128)(2,1)S(1)}, u32[]{:S(2)}, u32[]{:S(2)}) collective-permute-start(bf16[3,1,10,2688]{3,2,1,0:T(8,128)(2,1)S(1)} %get-tuple-element.15), channel_id=1, source_target_pairs={{1,0},{2,1},{3,2},{4,3},{5,4},{6,5},{7,6},{9,8},{10,9},{11,10},{12... | collective-permute-start | bytes 483848 | tf_op jit(solution)/shard_map/ppermute | solution.py:20
  62.1 6.1 %copy-start.6 = (bf16[4,3,128,128]{3,2,0,1:T(8,128)(2,1)S(1)}, bf16[4,3,128,128]{3,2,0,1:T(8,128)(2,1)}, u32[]{:S(2)}) copy-start(bf16[4,3,128,128]{3,2,0,1:T(8,128)(2,1)} %get-tuple-element.39) | copy-start | bytes 1179652
  63.3 3.7 %copy-start.2 = (bf16[3,6,4,21,128]{4,3,2,1,0:T(8,128)(2,1)}, bf16[3,6,4,21,128]{4,3,2,1,0:T(8,128)(2,1)S(1)}, u32[]{:S(2)}) copy-start(bf16[3,6,4,21,128]{4,3,2,1,0:T(8,128)(2,1)S(1)} %reshape.166) | copy-start | bytes 1161220
  68.2 1.8 %copy-start.7 = (bf16[3,6,4,2688]{3,2,1,0:T(4,128)(2,1)S(1)}, bf16[3,6,4,2688]{3,2,1,0:T(4,128)(2,1)}, u32[]{:S(2)}) copy-start(bf16[3,6,4,2688]{3,2,1,0:T(4,128)(2,1)} %get-tuple-element.11) | copy-start | bytes 1161220
  68.2 1.8 %copy-start.8 = (bf16[3,6,4,2688]{3,2,1,0:T(4,128)(2,1)S(1)}, bf16[3,6,4,2688]{3,2,1,0:T(4,128)(2,1)}, u32[]{:S(2)}) copy-start(bf16[3,6,4,2688]{3,2,1,0:T(4,128)(2,1)} %get-tuple-element.12) | copy-start | bytes 1161220
  80.1 3.8 %copy-start.3 = (bf16[3,6,4,21,128]{4,3,2,1,0:T(8,128)(2,1)S(1)}, bf16[3,6,4,21,128]{4,3,2,1,0:T(8,128)(2,1)}, u32[]{:S(2)}) copy-start(bf16[3,6,4,21,128]{4,3,2,1,0:T(8,128)(2,1)} %copy-done.2) | copy-start | bytes 1161220
  89.2 3.8 %copy-start.9 = (bf16[3,4,1,2688]{3,1,0,2:T(4,128)(2,1)S(1)}, bf16[3,4,1,2688]{3,1,0,2:T(4,128)(2,1)}, u32[]{:S(2)}) copy-start(bf16[3,4,1,2688]{3,1,0,2:T(4,128)(2,1)} %stack_reshape.17) | copy-start | bytes 193540
  94.9 7.2 %all-to-all-start = ((bf16[4,2,1536]{2,1,0:T(2,128)(2,1)}), bf16[4,2,1536]{2,1,0:T(2,128)(2,1)S(1)}, u32[]{:S(2)}, u32[]{:S(2)}) async-start(bf16[4,2,1536]{2,1,0:T(2,128)(2,1)} %reshape.197), calls=%async_computation | async-start | bytes 49152 | tf_op jit(solution)/shard_map/all_to_all | solution.py:76
